TPU v7x, 128 devices: a whole 4x4x4 slice. The times are simulated.
128 devices in a mesh: dom: 128 (over z, y, x, core).
Axes of the slice: x: 4, y: 4, z: 4, core: 2. Of those that a mesh axis runs over, the one named last changes fastest.
Arguments:
- a_blocks: bfloat16 [3072, 64, 448], P('dom'), may hold values from -0.25 to 0.25
- p_blocks: bfloat16 [3072, 64, 1728], P('dom'), may hold values from -0.59765625 to 0.59765625
- cols_a: int32 [3072, 7], P('dom'), may hold values from 0 to 3071, as said below
- cols_p: int32 [3072, 27], P('dom'), may hold values from 0 to 383, as said below
Outputs:
- coarse_op: float32 [384, 64, 4032], P('dom')
Inputs may be any that keep to these rules, and one draw needn't show every extreme that they name: `cols_a`: row e lists e itself first, then 7 - 1 other distinct rows, all in the aggregates agg(e) - 1, agg(e) and agg(e) + 1, counted cyclically. `cols_p`: the 27 entries of a row are distinct aggregates within 15 of the row's own aggregate, counted cyclically.
All inputs are finite; a program needn't handle non-finite values.
Results may differ from a plain program's by a relative error of at most 0.0041.
Values may be sent and summed in bfloat16 or wider, within the bound.
A program may use at most 192 MiB of HBM per device.

v0:
```python
import functools

import jax
import jax.numpy as jnp
from jax import lax
from jax.experimental import pallas as pl
from jax.experimental.pallas import tpu as pltpu
from jax.sharding import PartitionSpec as P

BS = 64
KA = 7
KP = 27
AGG = 8
H = 15
NC = 3
NB = 24
WIN = 31
BAND = 63
REACH = 5
MESH = pl.DeviceIdType.MESH

ROWS = AGG * BS
FRAME = 36 * BS
SLAB = 32 * BS
WIDE = 48 * BS
TOTAL = 66 * BS
WIDTHS = [36 * BS, 40 * BS, 42 * BS, 46 * BS, 48 * BS]
GROUP = NC * BS
CHUNK = 256
F32 = jnp.float32
BF16 = jnp.bfloat16


def tables(cols_a, cols_p, device, count_agg):
    odd = device % 2
    agg_here = jnp.arange(NB, dtype=jnp.int32) // AGG
    slot = (cols_p - (device * NC + agg_here)[:, None] + H) % count_agg
    frame = slot + agg_here[:, None] + 1 + odd
    slab = slot + (1 - odd)
    target = jnp.concatenate([frame, slab[:AGG], slab[NB - AGG :]], axis=0)

    def tile_of(target, count, blocks, tiles):
        spots = jnp.arange(count, dtype=jnp.int32)
        order = jnp.arange(blocks, dtype=jnp.int32)
        hit = target[:, :, None] == spots[None, None, :]
        found = blocks + jnp.sum(jnp.where(hit, order[None, :, None] - blocks, 0), axis=1)
        return ((found ^ spots[None, :]) & 1) * tiles + (found >> 1)

    fine = (cols_a - ((device * NC + agg_here - 1) * AGG)[:, None]) % (count_agg * AGG)
    p_tile = tile_of(target, 36, KP, 14)
    a_tile = tile_of(fine, 24, KA, 4)
    return jnp.concatenate([p_tile, jnp.pad(a_tile, ((0, 0), (0, 12)))], axis=0)


def swap_halves(x):
    return jnp.concatenate([x[:, BS:], x[:, :BS]], axis=1)


def band_kernel(tab, p_ref, a_ref, own_ref, slab_ref, turned_ref, dense_ref, p2, a2):
    agg = pl.program_id(0)
    low = lax.broadcasted_iota(jnp.int32, (BS, 128), 1) < BS

    def double(src, dst, wide, tiles):
        def step(e, _):
            dst[e, :, :wide] = src[e]
            dst[e, :, wide : 128 * tiles] = jnp.zeros((BS, 128 * tiles - wide), BF16)
            for tile in range(tiles):
                here = dst[e, :, 128 * tile : 128 * tile + 128]
                dst[e, :, 128 * (tiles + tile) : 128 * (tiles + tile + 1)] = swap_halves(here)
            return 0

        lax.fori_loop(0, AGG, step, 0)

    double(p_ref, p2, KP * BS, 14)
    double(a_ref, a2, KA * BS, 4)

    def place(src, dst, first, pairs):
        def step(e, _):
            for pair in range(pairs):
                left = pl.multiple_of(tab[first + e, 2 * pair] * 128, 128)
                right = pl.multiple_of(tab[first + e, 2 * pair + 1] * 128, 128)
                both = jnp.where(low, src[e, :, pl.ds(left, 128)], src[e, :, pl.ds(right, 128)])
                dst[e, :, 128 * pair : 128 * pair + 128] = both
            return 0

        lax.fori_loop(0, AGG, step, 0)

    @pl.when(agg != 1)
    def _():
        place(p2, slab_ref, NB + 4 * agg, 16)

    place(p2, own_ref, AGG * agg, 18)
    place(a2, dense_ref, NB + 2 * AGG + AGG * agg, 12)
    for tile in range(18):
        here = own_ref[:, :, 128 * tile : 128 * tile + 128].reshape(ROWS, 128)
        turned_ref[128 * tile : 128 * tile + 128, :] = here.T


def band(tab, p_blocks, a_blocks):
    return pl.pallas_call(
        band_kernel,
        out_shape=(
            jax.ShapeDtypeStruct((NB, BS, FRAME), BF16),
            jax.ShapeDtypeStruct((2 * AGG, BS, SLAB), BF16),
            jax.ShapeDtypeStruct((FRAME, NB * BS), BF16),
            jax.ShapeDtypeStruct((NB, BS, 3 * ROWS), BF16),
        ),
        grid_spec=pltpu.PrefetchScalarGridSpec(
            num_scalar_prefetch=1,
            grid=(NC,),
            in_specs=[
                pl.BlockSpec((AGG, BS, KP * BS), lambda i, t: (i, 0, 0)),
                pl.BlockSpec((AGG, BS, KA * BS), lambda i, t: (i, 0, 0)),
            ],
            out_specs=[
                pl.BlockSpec((AGG, BS, FRAME), lambda i, t: (i, 0, 0)),
                pl.BlockSpec((AGG, BS, SLAB), lambda i, t: (i // 2, 0, 0)),
                pl.BlockSpec((FRAME, ROWS), lambda i, t: (0, i)),
                pl.BlockSpec((AGG, BS, 3 * ROWS), lambda i, t: (i, 0, 0)),
            ],
            scratch_shapes=[
                pltpu.VMEM((AGG, BS, 2 * 14 * 128), BF16),
                pltpu.VMEM((AGG, BS, 2 * 4 * 128), BF16),
            ],
        ),
        compiler_params=pltpu.CompilerParams(vmem_limit_bytes=48 * 2**20),
    )(tab, p_blocks, a_blocks)


def dot(a, b):
    return jnp.dot(a, b, preferred_element_type=F32)


def chain_kernel(
    count, own, slab, turned, dense, out,
    ext, pt, ad, w, wf, part, rb, lb, tot,
    load_sem, halo_send, halo_recv, send_r, recv_r, send_l, recv_l,
):
    me = lax.axis_index("dom")
    right, left = lax.rem(me + 1, count), lax.rem(me + count - 1, count)
    odd = lax.rem(me, 2)

    barrier = pltpu.get_barrier_semaphore()
    for neighbour in (left, right):
        pl.semaphore_signal(barrier, inc=1, device_id=(neighbour,), device_id_type=MESH)
    pl.semaphore_wait(barrier, 2)

    halos = [
        pltpu.make_async_remote_copy(
            src_ref=slab.at[pl.ds(ROWS, ROWS)],
            dst_ref=ext.at[pl.ds(0, ROWS), pl.ds(0, SLAB)],
            send_sem=halo_send.at[0],
            recv_sem=halo_recv.at[0],
            device_id=(right,),
            device_id_type=MESH,
        ),
        pltpu.make_async_remote_copy(
            src_ref=slab.at[pl.ds(0, ROWS)],
            dst_ref=ext.at[pl.ds(4 * ROWS, ROWS), pl.ds(4 * BS, SLAB)],
            send_sem=halo_send.at[1],
            recv_sem=halo_recv.at[1],
            device_id=(left,),
            device_id_type=MESH,
        ),
    ]
    for copy in halos:
        copy.start()
    loads = [
        pltpu.make_async_copy(own, ext.at[pl.ds(ROWS, 3 * ROWS)], load_sem.at[0]),
        pltpu.make_async_copy(dense, ad, load_sem.at[1]),
        pltpu.make_async_copy(turned, pt, load_sem.at[2]),
    ]
    for copy in loads:
        copy.start()

    ext[:ROWS, SLAB:] = jnp.zeros((ROWS, FRAME - SLAB), BF16)
    ext[4 * ROWS :, : 4 * BS] = jnp.zeros((ROWS, 4 * BS), BF16)
    for step in range(1, REACH):
        before, after = WIDTHS[step - 1], WIDTHS[step]
        rb[step, :, before:after] = jnp.zeros((GROUP, after - before), BF16)
        lb[step, :, WIDE - after : WIDE - before] = jnp.zeros((GROUP, after - before), BF16)

    def chunks(body):
        def step(n, _):
            body(pl.multiple_of(n * CHUNK, CHUNK))
            return 0

        lax.fori_loop(0, FRAME // CHUNK, step, 0)

    loads[0].wait()
    loads[1].wait()

    def inner(at):
        cols = pl.ds(at, CHUNK)
        w[ROWS : 2 * ROWS, cols] = dot(ad[ROWS : 2 * ROWS, :], ext[ROWS : 4 * ROWS, cols]).astype(BF16)
        wf[:ROWS, cols] = dot(ad[:ROWS, ROWS:], ext[ROWS : 3 * ROWS, cols])
        wf[ROWS:, cols] = dot(ad[2 * ROWS :, : 2 * ROWS], ext[2 * ROWS : 4 * ROWS, cols])

    chunks(inner)
    loads[2].wait()
    halos[0].wait_recv()

    def first(at):
        cols = pl.ds(at, CHUNK)
        more = dot(ad[:ROWS, :ROWS], ext[:ROWS, cols])
        w[:ROWS, cols] = (wf[:ROWS, cols] + more).astype(BF16)

    chunks(first)
    halos[1].wait_recv()

    def last(at):
        cols = pl.ds(at, CHUNK)
        more = dot(ad[2 * ROWS :, 2 * ROWS :], ext[4 * ROWS :, cols])
        w[2 * ROWS :, cols] = (wf[ROWS:, cols] + more).astype(BF16)

    chunks(last)

    def product(group, at):
        rows = pl.ds(pl.multiple_of((NC * group + 1 + odd) * BS, BS), GROUP)
        return dot(pt[rows, :], w[:, pl.ds(at, CHUNK)]).astype(BF16)

    def send(step):
        width = WIDTHS[step]
        pair = []
        for buf, begin, sends, recvs, target in (
            (rb, 0, send_r, recv_r, right),
            (lb, WIDE - width, send_l, recv_l, left),
        ):
            copy = pltpu.make_async_remote_copy(
                src_ref=buf.at[step, :, pl.ds(begin, width)],
                dst_ref=buf.at[step + 1, :, pl.ds(begin, width)],
                send_sem=sends.at[step],
                recv_sem=recvs.at[step],
                device_id=(target,),
                device_id_type=MESH,
            )
            copy.start()
            pair.append(copy)
        return pair

    def ends(at):
        cols = pl.ds(at, CHUNK)
        rb[0, :, cols] = product(2 * REACH, at)
        lb[0, :, pl.ds(pl.multiple_of(at + WIDE - FRAME, 128), CHUNK)] = product(0, at)

    chunks(ends)
    sent = [send(0)]
    for step in range(1, REACH):
        reach = REACH - step

        def both(at):
            cols = pl.ds(at, CHUNK)
            part[0, :, cols] = product(REACH + reach, at)
            part[1, :, cols] = product(REACH - reach, at)

        chunks(both)
        if step % 2:
            shift_r = 3 * step + 1 - 2 * odd
            shift_l = 12 - (3 * step - 1 + 2 * odd)
        else:
            shift_r, shift_l = 3 * step, 12 - 3 * step
        for side, (buf, shift) in enumerate(((rb, shift_r), (lb, shift_l))):
            sent[step - 1][side].wait_recv()

            def add(at):
                cols = pl.ds(pl.multiple_of(at + shift * BS, 128), CHUNK)
                summed = buf[step, :, cols].astype(F32) + part[side, :, pl.ds(at, CHUNK)].astype(F32)
                buf[step, :, cols] = summed.astype(BF16)

            chunks(add)
        sent.append(send(step))

    def middle(at):
        part[0, :, pl.ds(at, CHUNK)] = product(REACH, at)

    chunks(middle)
    tot[:, : 18 * BS] = jnp.zeros((GROUP, 18 * BS), F32)
    tot[:, 52 * BS :] = jnp.zeros((GROUP, 14 * BS), F32)
    tot[:, 18 * BS : 52 * BS] = jnp.zeros((GROUP, 34 * BS), F32)

    def put(at):
        cols = pl.ds(pl.multiple_of(at + (16 - 2 * odd) * BS, 128), CHUNK)
        tot[:, cols] = part[0, :, pl.ds(at, CHUNK)].astype(F32)

    chunks(put)
    sent[REACH - 1][0].wait_recv()
    tot[:, :WIDE] += rb[REACH].astype(F32)
    sent[REACH - 1][1].wait_recv()
    tot[:, 18 * BS :] += lb[REACH].astype(F32)
    for parity in (0, 1):

        @pl.when(odd == parity)
        def _():
            for row in range(NC):
                start = (row + 1 - parity) * BS
                out[row] = tot[row * BS : (row + 1) * BS, start : start + BAND * BS]

    for copy in halos:
        copy.wait_send()
    for pair in sent:
        for copy in pair:
            copy.wait_send()


def chain(count, own, slab, turned, dense):
    anywhere = pl.BlockSpec(memory_space=pl.ANY)
    return pl.pallas_call(
        functools.partial(chain_kernel, count),
        out_shape=jax.ShapeDtypeStruct((NC, BS, BAND * BS), F32),
        in_specs=[anywhere] * 4,
        out_specs=pl.BlockSpec(memory_space=pltpu.VMEM),
        scratch_shapes=[
            pltpu.VMEM((5 * ROWS, FRAME), BF16),
            pltpu.VMEM((FRAME, 3 * ROWS), BF16),
            pltpu.VMEM((3 * ROWS, 3 * ROWS), BF16),
            pltpu.VMEM((3 * ROWS, FRAME), BF16),
            pltpu.VMEM((2 * ROWS, FRAME), F32),
            pltpu.VMEM((2, GROUP, FRAME), BF16),
            pltpu.VMEM((REACH + 1, GROUP, WIDE), BF16),
            pltpu.VMEM((REACH + 1, GROUP, WIDE), BF16),
            pltpu.VMEM((GROUP, TOTAL), F32),
            pltpu.SemaphoreType.DMA((3,)),
            pltpu.SemaphoreType.DMA((2,)),
            pltpu.SemaphoreType.DMA((2,)),
            pltpu.SemaphoreType.DMA((REACH,)),
            pltpu.SemaphoreType.DMA((REACH,)),
            pltpu.SemaphoreType.DMA((REACH,)),
            pltpu.SemaphoreType.DMA((REACH,)),
        ],
        compiler_params=pltpu.CompilerParams(
            collective_id=0, has_side_effects=True, vmem_limit_bytes=63 * 2**20
        ),
    )(own, slab, turned, dense)


def body(a_blocks, p_blocks, cols_a, cols_p):
    count = lax.axis_size("dom")
    tab = tables(cols_a, cols_p, lax.axis_index("dom"), NC * count)
    own, slab, turned, dense = band(tab, p_blocks, a_blocks)
    return chain(
        count,
        own.reshape(3 * ROWS, FRAME),
        slab.reshape(2 * ROWS, SLAB),
        turned,
        dense.reshape(3 * ROWS, 3 * ROWS),
    )


def solution(mesh):
    in_specs = (P("dom", None, None), P("dom", None, None), P("dom", None), P("dom", None))
    out_specs = P("dom", None, None)
    return jax.shard_map(body, mesh=mesh, in_specs=in_specs, out_specs=out_specs, check_vma=False)
```

profile of v0, /device:TPU:0, one launch (start us, length us, event | category | flops | bytes accessed | tf_op | source)
XLA Modules:
  0.0 155.7 jit_solution(6104637976335686866)
XLA Ops:
  0.0 0.7 add_select_fusion.1
  0.7 0.1 select_reduce_fusion.1
  0.8 0.8 add_add_fusion
  1.7 0.1 copy.6
  1.7 0.2 select_reduce_fusion
  2.0 0.0 copy-start.1
  2.0 1.4 copy-done.1
  3.4 19.2 %shard_map.46 = (bf16[24,64,2304]{2,1,0:T(8,128)(2,1)}, bf16[16,64,2048]{2,1,0:T(8,128)(2,1)S(1)}, bf16[2304,1536]{1,0:T(8,128)(2,1)}, bf16[24,64,1536]{2,1,0:T(8,128)(2,1)}) custom-call(s32[64,36]{1,0:T(8,128)S(1)} %pad_add_fusion.tab, bf16[24,64,1728]{2,1,0:T(8,128)(2,1)} %p_ref.1, bf16[24,64,448]{2,1,0:T(8,128)(2,1)S(1)} %copy-done.1), custom_call_target="tpu_custom_call" | custom-call | tf_op jit(solution)/shard_map/pallas_call | solution.py:100
  22.6 0.0 copy-start
  22.6 2.0 %copy-done = bf16[16,64,2048]{2,1,0:T(8,128)(2,1)} copy-done((bf16[16,64,2048]{2,1,0:T(8,128)(2,1)}, bf16[16,64,2048]{2,1,0:T(8,128)(2,1)S(1)}, u32[]{:S(2)}) %copy-start) | copy-done | bytes 4194328
  24.6 127.2 %shard_map.47 = f32[3,64,4032]{2,1,0:T(8,128)} custom-call(bf16[1536,2304]{1,0:T(8,128)(2,1)} %bitcast.4, bf16[1024,2048]{1,0:T(8,128)(2,1)} %bitcast.3, bf16[2304,1536]{1,0:T(8,128)(2,1)} %get-tuple-element.11.turned, bf16[1536,1536]{1,0:T(8,128)(2,1)} %bitcast.5), custom_call_target="tpu_custom_call" | custom-call | tf_op jit(solution)/shard_map/pallas_call | solution.py:307
  151.8 3.9 %copy.8 = f32[3,64,4032]{2,1,0:T(8,128)} copy(f32[3,64,4032]{2,1,0:T(8,128)} %shard_map.47) | data formatting | bytes 6193152
  (9 shorter events, 0.0 us)
Async XLA Ops:
  2.0 1.4 copy-start.1
  22.6 2.0 %copy-start = (bf16[16,64,2048]{2,1,0:T(8,128)(2,1)}, bf16[16,64,2048]{2,1,0:T(8,128)(2,1)S(1)}, u32[]{:S(2)}) copy-start(bf16[16,64,2048]{2,1,0:T(8,128)(2,1)S(1)} %get-tuple-element.10) | copy-start | bytes 12582916
where the time goes:
time: 156 us
  Pallas kernels  146 us (94%)
  local copies, waits for them, and re-layouts  7.37 us (5%)
  other arithmetic  1.88 us (1%)
    pallas_call x1, Pallas kernels, chain(): pl.pallas_call(functools.partial(chain_kernel, count), out_shape=jax.Shap...  127 us
    pallas_call x1, Pallas kernels, band(): pl.pallas_call(band_kernel, out_shape=(jax.ShapeDtypeStruct((NB, BS, FRAM...  19.2 us
    unnamed x5, local copies, waits for them, and re-layouts  7.29 us

commit v1 on v0

v1 whole, which is shorter than its diff:
```python
import functools

import jax
import jax.numpy as jnp
from jax import lax
from jax.experimental import pallas as pl
from jax.experimental.pallas import tpu as pltpu
from jax.sharding import PartitionSpec as P

BS = 64
KA = 7
KP = 27
AGG = 8
H = 15
NC = 3
NB = 24
WIN = 31
BAND = 63
REACH = 5
MESH = pl.DeviceIdType.MESH

ROWS = AGG * BS
FRAME = 36 * BS
SLAB = 32 * BS
WIDE = 48 * BS
TOTAL = 66 * BS
WIDTHS = [36 * BS, 40 * BS, 42 * BS, 46 * BS, 48 * BS]
GROUP = NC * BS
CHUNK = 768
F32 = jnp.float32
BF16 = jnp.bfloat16


def tables(cols_a, cols_p, device, count_agg):
    odd = device % 2
    agg_here = jnp.arange(NB, dtype=jnp.int32) // AGG
    slot = (cols_p - (device * NC + agg_here)[:, None] + H) % count_agg
    frame = slot + agg_here[:, None] + 1 + odd
    slab = slot + (1 - odd)
    target = jnp.concatenate([frame, slab[:AGG], slab[NB - AGG :]], axis=0)

    def tile_of(target, count, blocks, tiles):
        spots = jnp.arange(count, dtype=jnp.int32)
        order = jnp.arange(blocks, dtype=jnp.int32)
        hit = target[:, :, None] == spots[None, None, :]
        found = blocks + jnp.sum(jnp.where(hit, order[None, :, None] - blocks, 0), axis=1)
        return ((found ^ spots[None, :]) & 1) * tiles + (found >> 1)

    fine = (cols_a - ((device * NC + agg_here - 1) * AGG)[:, None]) % (count_agg * AGG)
    p_tile = tile_of(target, 36, KP, 14)
    a_tile = tile_of(fine, 24, KA, 4)
    return jnp.concatenate([p_tile, jnp.pad(a_tile, ((0, 0), (0, 12)))], axis=0)


def swap_halves(x):
    return jnp.concatenate([x[:, BS:], x[:, :BS]], axis=1)


def dot(a, b):
    return jnp.dot(a, b, preferred_element_type=F32)


def aligned(value, multiple=128):
    return pl.multiple_of(value, multiple)


def doubled(src, first, dst, wide, tiles):
    def step(e, _):
        rows = pl.ds(aligned(e * BS, BS), BS)
        for tile in range(tiles):
            if 128 * (tile + 1) <= wide:
                here = src[first + e, :, 128 * tile : 128 * tile + 128]
            else:
                here = jnp.concatenate([src[first + e, :, 128 * tile : wide], jnp.zeros((BS, BS), BF16)], axis=1)
            dst[tile, rows, :] = here
            dst[tiles + tile, rows, :] = swap_halves(here)
        return 0

    lax.fori_loop(0, AGG, step, 0)


def place(tab, first, src, dst, dst_row, pairs):
    low = lax.broadcasted_iota(jnp.int32, (BS, 128), 1) < BS

    def step(e, _):
        rows = pl.ds(aligned(e * BS, BS), BS)
        to = pl.ds(aligned(dst_row + e * BS, BS), BS)
        for pair in range(pairs):
            left = src[tab[first + e, 2 * pair], rows, :]
            right = src[tab[first + e, 2 * pair + 1], rows, :]
            dst[to, 128 * pair : 128 * pair + 128] = jnp.where(low, left, right)
        return 0

    lax.fori_loop(0, AGG, step, 0)


def chain_kernel(count, tab, p_blocks, a_blocks, from_left, from_right, middle, *scratch):
    raw, raw_a, p2, a2, slab, ext, pt, ad, w, wf, part = scratch[:11]
    rb = [*scratch[11 : 11 + REACH], from_left]
    lb = [*scratch[11 + REACH : 11 + 2 * REACH], from_right]
    load_sem, halo_send, halo_recv, send_r, recv_r, send_l, recv_l = scratch[11 + 2 * REACH :]
    me = lax.axis_index("dom")
    odd = lax.rem(me, 2)
    right, left = lax.rem(me + 1, count), lax.rem(me + count - 1, count)
    far, near = lax.rem(me + count - 1 + 2 * odd, count), lax.rem(me + count + 1 - 2 * odd, count)
    far_agg, near_agg = 2 * odd, 2 - 2 * odd

    def load(agg, slot, sem):
        return pltpu.make_async_copy(p_blocks.at[pl.ds(AGG * agg, AGG)], raw.at[slot], load_sem.at[sem])

    loads = [load(far_agg, 0, 0), load(near_agg, 1, 1)]
    load_a = pltpu.make_async_copy(a_blocks, raw_a, load_sem.at[2])
    for copy in (*loads, load_a):
        copy.start()
    barrier = pltpu.get_barrier_semaphore()
    for neighbour in (left, right):
        pl.semaphore_signal(barrier, inc=1, device_id=(neighbour,), device_id_type=MESH)

    def halo(side, target, edge):
        return pltpu.make_async_remote_copy(
            src_ref=slab.at[side],
            dst_ref=ext.at[pl.ds(aligned(edge * 4 * ROWS), ROWS), pl.ds(aligned(edge * 4 * BS), SLAB)],
            send_sem=halo_send.at[side],
            recv_sem=halo_recv.at[side],
            device_id=(target,),
            device_id_type=MESH,
        )

    halos = [halo(0, far, 1 - odd), halo(1, near, odd)]

    def own(agg):
        place(tab, AGG * agg, p2, ext, ROWS + ROWS * agg, 18)

    loads[0].wait()
    doubled(raw.at[0], 0, p2, KP * BS, 14)
    place(tab, NB + 4 * far_agg, p2, slab.at[0], 0, 16)
    pl.semaphore_wait(barrier, 2)
    halos[0].start()
    inner_load = load(1, 0, 3)
    inner_load.start()
    own(far_agg)
    loads[1].wait()
    doubled(raw.at[1], 0, p2, KP * BS, 14)
    place(tab, NB + 4 * near_agg, p2, slab.at[1], 0, 16)
    halos[1].start()
    own(near_agg)
    inner_load.wait()
    doubled(raw.at[0], 0, p2, KP * BS, 14)
    own(1)
    load_a.wait()
    for agg in range(NC):
        doubled(raw_a, AGG * agg, a2, KA * BS, 4)
        place(tab, NB + 2 * AGG + AGG * agg, a2, ad, ROWS * agg, 12)

    ext[:ROWS, SLAB:] = jnp.zeros((ROWS, FRAME - SLAB), BF16)
    ext[4 * ROWS :, : 4 * BS] = jnp.zeros((ROWS, 4 * BS), BF16)
    for step in range(1, REACH):
        before, after = WIDTHS[step - 1], WIDTHS[step]
        rb[step][:, before:after] = jnp.zeros((GROUP, after - before), BF16)
        lb[step][:, : after - before] = jnp.zeros((GROUP, after - before), BF16)

    for agg in range(NC):

        def turn(tile, _):
            lanes = pl.ds(aligned(tile * 128), 128)
            pt[lanes, ROWS * agg : ROWS * (agg + 1)] = ext[ROWS * (agg + 1) : ROWS * (agg + 2), lanes].T
            return 0

        lax.fori_loop(0, FRAME // 128, turn, 0)

    def chunks(body):
        def step(n, _):
            body(aligned(n * CHUNK))
            return 0

        lax.fori_loop(0, FRAME // CHUNK, step, 0)

    far_rows = pl.ds(aligned(far_agg * ROWS), ROWS)
    near_rows = pl.ds(aligned(near_agg * ROWS), ROWS)

    def inner(at):
        cols = pl.ds(at, CHUNK)
        w[ROWS : 2 * ROWS, cols] = dot(ad[ROWS : 2 * ROWS, :], ext[ROWS : 4 * ROWS, cols]).astype(BF16)
        wf[:, cols] = dot(
            ad[far_rows, pl.ds(aligned(ROWS * (1 - odd)), 2 * ROWS)],
            ext[pl.ds(aligned(ROWS + ROWS * odd), 2 * ROWS), cols],
        )

    def near_side(at):
        cols = pl.ds(at, CHUNK)
        whole = dot(ad[near_rows, :], ext[pl.ds(aligned(2 * ROWS * (1 - odd)), 3 * ROWS), cols])
        w[near_rows, cols] = whole.astype(BF16)

    def far_side(at):
        cols = pl.ds(at, CHUNK)
        more = dot(
            ad[far_rows, pl.ds(aligned(2 * ROWS * odd), ROWS)],
            ext[pl.ds(aligned(4 * ROWS * odd), ROWS), cols],
        )
        w[far_rows, cols] = (wf[:, cols] + more).astype(BF16)

    chunks(inner)
    halos[1].wait_recv()
    chunks(near_side)
    halos[0].wait_recv()
    chunks(far_side)

    def product(group, at):
        rows = pl.ds(aligned((NC * group + 1 + odd) * BS, BS), GROUP)
        return dot(pt[rows, :], w[:, pl.ds(at, CHUNK)]).astype(BF16)

    def send(step):
        width = WIDTHS[step]
        begin = WIDTHS[min(step + 1, REACH - 1)] - width
        pair = []
        for buf, place_to, sends, recvs, target in (
            (rb, 0, send_r, recv_r, right),
            (lb, begin, send_l, recv_l, left),
        ):
            copy = pltpu.make_async_remote_copy(
                src_ref=buf[step],
                dst_ref=buf[step + 1].at[:, pl.ds(place_to, width)],
                send_sem=sends.at[step],
                recv_sem=recvs.at[step],
                device_id=(target,),
                device_id_type=MESH,
            )
            copy.start()
            pair.append(copy)
        return pair

    def ends(at):
        cols = pl.ds(at, CHUNK)
        rb[0][:, cols] = product(2 * REACH, at)
        lb[0][:, cols] = product(0, at)

    chunks(ends)
    sent = [send(0)]
    for step in range(1, REACH):
        reach = REACH - step

        def both(at):
            cols = pl.ds(at, CHUNK)
            part[0, :, cols] = product(REACH + reach, at)
            part[1, :, cols] = product(REACH - reach, at)

        chunks(both)
        spare = WIDTHS[step] // BS - 36
        if step % 2:
            shift_r = 3 * step + 1 - 2 * odd
            shift_l = spare - (3 * step - 1 + 2 * odd)
        else:
            shift_r, shift_l = 3 * step, spare - 3 * step
        for side, (buf, shift) in enumerate(((rb[step], shift_r), (lb[step], shift_l))):
            sent[step - 1][side].wait_recv()

            def add(at):
                cols = pl.ds(aligned(at + shift * BS), CHUNK)
                summed = buf[:, cols].astype(F32) + part[side, :, pl.ds(at, CHUNK)].astype(F32)
                buf[:, cols] = summed.astype(BF16)

            chunks(add)
        sent.append(send(step))

    def centre(at):
        part[0, :, pl.ds(at, CHUNK)] = product(REACH, at)

    chunks(centre)
    keep = pltpu.make_async_copy(part.at[0], middle, load_sem.at[4])
    keep.start()
    for pair in sent:
        for copy in pair:
            copy.wait_send()
    for copy in halos:
        copy.wait_send()
    keep.wait()
    for copy in sent[-1]:
        copy.wait_recv()


def chain(count, tab, p_blocks, a_blocks):
    anywhere = pl.BlockSpec(memory_space=pl.ANY)
    sums = [pltpu.VMEM((GROUP, width), BF16) for width in WIDTHS]
    return pl.pallas_call(
        functools.partial(chain_kernel, count),
        out_shape=(
            jax.ShapeDtypeStruct((GROUP, WIDE), BF16),
            jax.ShapeDtypeStruct((GROUP, WIDE), BF16),
            jax.ShapeDtypeStruct((GROUP, FRAME), BF16),
        ),
        in_specs=[pl.BlockSpec(memory_space=pltpu.SMEM), anywhere, anywhere],
        out_specs=[anywhere] * 3,
        scratch_shapes=[
            pltpu.VMEM((2, AGG, BS, KP * BS), BF16),
            pltpu.VMEM((NB, BS, KA * BS), BF16),
            pltpu.VMEM((2 * 14, ROWS, 128), BF16),
            pltpu.VMEM((2 * 4, ROWS, 128), BF16),
            pltpu.VMEM((2, ROWS, SLAB), BF16),
            pltpu.VMEM((5 * ROWS, FRAME), BF16),
            pltpu.VMEM((FRAME, 3 * ROWS), BF16),
            pltpu.VMEM((3 * ROWS, 3 * ROWS), BF16),
            pltpu.VMEM((3 * ROWS, FRAME), BF16),
            pltpu.VMEM((ROWS, FRAME), F32),
            pltpu.VMEM((2, GROUP, FRAME), BF16),
            *sums,
            *sums,
            pltpu.SemaphoreType.DMA((5,)),
            pltpu.SemaphoreType.DMA((2,)),
            pltpu.SemaphoreType.DMA((2,)),
            pltpu.SemaphoreType.DMA((REACH,)),
            pltpu.SemaphoreType.DMA((REACH,)),
            pltpu.SemaphoreType.DMA((REACH,)),
            pltpu.SemaphoreType.DMA((REACH,)),
        ],
        compiler_params=pltpu.CompilerParams(
            collective_id=0, has_side_effects=True, vmem_limit_bytes=63 * 2**20
        ),
    )(tab, p_blocks, a_blocks)


def gather_kernel(left_ref, right_ref, middle_ref, out_ref, tot):
    odd = lax.rem(lax.axis_index("dom"), 2)
    tot[:, :WIDE] = left_ref[...].astype(F32)
    tot[:, WIDE:] = jnp.zeros((BS, TOTAL - WIDE), F32)
    own = pl.ds(aligned((16 - 2 * odd) * BS), FRAME)
    tot[:, own] += middle_ref[...].astype(F32)
    tot[:, TOTAL - WIDE :] += right_ref[...].astype(F32)
    first = pl.program_id(0) + 1 - odd
    for start in range(NC + 1):

        @pl.when(first == start)
        def _():
            out_ref[0] = tot[:, start * BS : (start + BAND) * BS]


def gather(from_left, from_right, middle):
    return pl.pallas_call(
        gather_kernel,
        out_shape=jax.ShapeDtypeStruct((NC, BS, BAND * BS), F32),
        grid=(NC,),
        in_specs=[
            pl.BlockSpec((BS, WIDE), lambda i: (i, 0)),
            pl.BlockSpec((BS, WIDE), lambda i: (i, 0)),
            pl.BlockSpec((BS, FRAME), lambda i: (i, 0)),
        ],
        out_specs=pl.BlockSpec((1, BS, BAND * BS), lambda i: (i, 0, 0)),
        scratch_shapes=[pltpu.VMEM((BS, TOTAL), F32)],
    )(from_left, from_right, middle)


def body(a_blocks, p_blocks, cols_a, cols_p):
    count = lax.axis_size("dom")
    tab = tables(cols_a, cols_p, lax.axis_index("dom"), NC * count)
    return gather(*chain(count, tab, p_blocks, a_blocks))


def solution(mesh):
    in_specs = (P("dom", None, None), P("dom", None, None), P("dom", None), P("dom", None))
    out_specs = P("dom", None, None)
    return jax.shard_map(body, mesh=mesh, in_specs=in_specs, out_specs=out_specs, check_vma=False)
```

time: 156 us -> 132 us (0.85)
  Pallas kernels: 146 us -> 129 us
  local copies, waits for them, and re-layouts: 7.37 us -> 0.08 us
    pallas_call x2, Pallas kernels: 146 us -> 129 us  [the longest x1 123 us: chain(): pl.pallas_call(functools.partial(chain_kernel, count), out_shape=(jax.Sha...]
    unnamed x5 -> x0, local copies, waits for them, and re-layouts: 7.29 us -> none
where the time goes in v1:
time: 132 us; the launch traced here: 131 us
  Pallas kernels  129 us (98%)
  other arithmetic  2.5 us (2%)
    pallas_call x1, Pallas kernels, chain(): pl.pallas_call(functools.partial(chain_kernel, count), out_shape=(jax.Sha...  123 us
    pallas_call x1, Pallas kernels, gather(): pl.pallas_call(gather_kernel, out_shape=jax.ShapeDtypeStruct((NC, BS, BAN...  5.22 us

profile of v1, /device:TPU:0, one launch (start us, length us, event | category | flops | bytes accessed | tf_op | source)
XLA Modules:
  0.0 131.3 jit_solution(11461197222584780366)
XLA Ops:
  0.0 0.7 add_select_fusion.1
  0.7 0.1 select_reduce_fusion.1
  0.8 0.8 add_add_fusion
  1.7 0.1 copy.6
  1.7 0.2 select_reduce_fusion
  2.0 0.6 pad_add_fusion.tab
  2.6 123.4 %shard_map.46 = (bf16[192,3072]{1,0:T(8,128)(2,1)}, bf16[192,3072]{1,0:T(8,128)(2,1)}, bf16[192,2304]{1,0:T(8,128)(2,1)}) custom-call(s32[64,36]{1,0:T(8,128)} %pad_add_fusion.tab, bf16[24,64,1728]{2,1,0:T(8,128)(2,1)} %p_blocks.1, bf16[24,64,448]{2,1,0:T(8,128)(2,1)} %a_blocks.1), custom_call_target="tpu_custom_call" | custom-call | tf_op jit(solution)/shard_map/pallas_call | solution.py:284
  126.1 5.2 %shard_map.47 = f32[3,64,4032]{2,1,0:T(8,128)} custom-call(bf16[192,3072]{1,0:T(8,128)(2,1)} %get-tuple-element.8.left_ref, bf16[192,3072]{1,0:T(8,128)(2,1)} %get-tuple-element.9.right_ref, bf16[192,2304]{1,0:T(8,128)(2,1)} %get-tuple-element.10.middle_ref), custom_call_target="tpu_custom_call" | custom-call | tf_op jit(solution)/shard_map/pallas_call | solution.py:337
  (8 shorter events, 0.0 us)

commit v2 on v1

--- a/solution.py
+++ b/solution.py
@@ -24,7 +24,8 @@
 SLAB = 32 * BS
 WIDE = 48 * BS
 TOTAL = 66 * BS
-WIDTHS = [36 * BS, 40 * BS, 42 * BS, 46 * BS, 48 * BS]
+FAR_WIDTH, FAR_SHIFT = [36, 38, 42, 44, 48], [0, 2, 6, 8, 12]
+NEAR_WIDTH, NEAR_SHIFT = [36, 40, 42, 46, 48], [0, 4, 6, 10, 12]
 GROUP = NC * BS
 CHUNK = 768
 F32 = jnp.float32
@@ -94,14 +95,13 @@
     lax.fori_loop(0, AGG, step, 0)
 
 
-def chain_kernel(count, tab, p_blocks, a_blocks, from_left, from_right, middle, *scratch):
+def chain_kernel(count, tab, p_blocks, a_blocks, from_far, from_near, middle, *scratch):
     raw, raw_a, p2, a2, slab, ext, pt, ad, w, wf, part = scratch[:11]
-    rb = [*scratch[11 : 11 + REACH], from_left]
-    lb = [*scratch[11 + REACH : 11 + 2 * REACH], from_right]
-    load_sem, halo_send, halo_recv, send_r, recv_r, send_l, recv_l = scratch[11 + 2 * REACH :]
+    to_far = [*scratch[11 : 11 + REACH], from_near]
+    to_near = [*scratch[11 + REACH : 11 + 2 * REACH], from_far]
+    load_sem, halo_send, halo_recv, send_far, recv_far, send_near, recv_near = scratch[11 + 2 * REACH :]
     me = lax.axis_index("dom")
     odd = lax.rem(me, 2)
-    right, left = lax.rem(me + 1, count), lax.rem(me + count - 1, count)
     far, near = lax.rem(me + count - 1 + 2 * odd, count), lax.rem(me + count + 1 - 2 * odd, count)
     far_agg, near_agg = 2 * odd, 2 - 2 * odd
 
@@ -113,7 +113,7 @@
     for copy in (*loads, load_a):
         copy.start()
     barrier = pltpu.get_barrier_semaphore()
-    for neighbour in (left, right):
+    for neighbour in (far, near):
         pl.semaphore_signal(barrier, inc=1, device_id=(neighbour,), device_id_type=MESH)
 
     def halo(side, target, edge):
@@ -155,9 +155,11 @@
     ext[:ROWS, SLAB:] = jnp.zeros((ROWS, FRAME - SLAB), BF16)
     ext[4 * ROWS :, : 4 * BS] = jnp.zeros((ROWS, 4 * BS), BF16)
     for step in range(1, REACH):
-        before, after = WIDTHS[step - 1], WIDTHS[step]
-        rb[step][:, before:after] = jnp.zeros((GROUP, after - before), BF16)
-        lb[step][:, : after - before] = jnp.zeros((GROUP, after - before), BF16)
+        for buf, more, goes_right, before in (
+            (to_far, 2 * BS, odd, NEAR_WIDTH[step - 1]),
+            (to_near, 4 * BS, 1 - odd, FAR_WIDTH[step - 1]),
+        ):
+            buf[step][:, pl.ds(aligned(goes_right * before * BS), more)] = jnp.zeros((GROUP, more), BF16)
 
     for agg in range(NC):
 
@@ -209,58 +211,64 @@
         rows = pl.ds(aligned((NC * group + 1 + odd) * BS, BS), GROUP)
         return dot(pt[rows, :], w[:, pl.ds(at, CHUNK)]).astype(BF16)
 
-    def send(step):
-        width = WIDTHS[step]
-        begin = WIDTHS[min(step + 1, REACH - 1)] - width
-        pair = []
-        for buf, place_to, sends, recvs, target in (
-            (rb, 0, send_r, recv_r, right),
-            (lb, begin, send_l, recv_l, left),
-        ):
-            copy = pltpu.make_async_remote_copy(
-                src_ref=buf[step],
-                dst_ref=buf[step + 1].at[:, pl.ds(place_to, width)],
-                send_sem=sends.at[step],
-                recv_sem=recvs.at[step],
-                device_id=(target,),
-                device_id_type=MESH,
-            )
-            copy.start()
-            pair.append(copy)
-        return pair
-
-    def ends(at):
-        cols = pl.ds(at, CHUNK)
-        rb[0][:, cols] = product(2 * REACH, at)
-        lb[0][:, cols] = product(0, at)
-
-    chunks(ends)
-    sent = [send(0)]
-    for step in range(1, REACH):
-        reach = REACH - step
-
-        def both(at):
+    def send(step, far_side):
+        buf, lands = (to_far, to_near) if far_side else (to_near, to_far)
+        width = (FAR_WIDTH if far_side else NEAR_WIDTH)[step] * BS
+        grows = 0 if step == REACH - 1 else (4 * BS if far_side else 2 * BS)
+        goes_left = 1 - odd if far_side else odd
+        copy = pltpu.make_async_remote_copy(
+            src_ref=buf[step],
+            dst_ref=lands[step + 1].at[:, pl.ds(aligned(goes_left * grows), width)],
+            send_sem=(send_far if far_side else send_near).at[step],
+            recv_sem=(recv_far if far_side else recv_near).at[step],
+            device_id=(far if far_side else near,),
+            device_id_type=MESH,
+        )
+        copy.start()
+        return copy
+
+    def far_product(step, at):
+        return product(REACH + (REACH - step) * (2 * odd - 1), at)
+
+    def near_product(step, at):
+        return product(REACH - (REACH - step) * (2 * odd - 1), at)
+
+    def add(buf, shift, side):
+        def some(at):
+            cols = pl.ds(aligned(at + shift * BS), CHUNK)
+            summed = buf[:, cols].astype(F32) + part[side, :, pl.ds(at, CHUNK)].astype(F32)
+            buf[:, cols] = summed.astype(BF16)
+
+        chunks(some)
+
+    def far_first(at):
+        to_far[0][:, pl.ds(at, CHUNK)] = far_product(0, at)
+
+    def near_first(at):
+        to_near[0][:, pl.ds(at, CHUNK)] = near_product(0, at)
+
+    chunks(far_first)
+    far_sent = [send(0, True)]
+    chunks(near_first)
+    near_sent = [send(0, False)]
+    for step in range(REACH):
+
+        def prepare(at):
             cols = pl.ds(at, CHUNK)
-            part[0, :, cols] = product(REACH + reach, at)
-            part[1, :, cols] = product(REACH - reach, at)
-
-        chunks(both)
-        spare = WIDTHS[step] // BS - 36
-        if step % 2:
-            shift_r = 3 * step + 1 - 2 * odd
-            shift_l = spare - (3 * step - 1 + 2 * odd)
-        else:
-            shift_r, shift_l = 3 * step, spare - 3 * step
-        for side, (buf, shift) in enumerate(((rb[step], shift_r), (lb[step], shift_l))):
-            sent[step - 1][side].wait_recv()
-
-            def add(at):
-                cols = pl.ds(aligned(at + shift * BS), CHUNK)
-                summed = buf[:, cols].astype(F32) + part[side, :, pl.ds(at, CHUNK)].astype(F32)
-                buf[:, cols] = summed.astype(BF16)
-
-            chunks(add)
-        sent.append(send(step))
+            if step > 0:
+                part[1, :, cols] = near_product(step, at)
+            if step + 1 < REACH:
+                part[0, :, cols] = far_product(step + 1, at)
+
+        chunks(prepare)
+        if step > 0:
+            far_sent[step - 1].wait_recv()
+            add(to_near[step], NEAR_SHIFT[step] * (1 - odd), 1)
+            near_sent.append(send(step, False))
+        if step + 1 < REACH:
+            near_sent[step].wait_recv()
+            add(to_far[step + 1], FAR_SHIFT[step + 1] * odd, 0)
+            far_sent.append(send(step + 1, True))
 
     def centre(at):
         part[0, :, pl.ds(at, CHUNK)] = product(REACH, at)
@@ -268,19 +276,16 @@
     chunks(centre)
     keep = pltpu.make_async_copy(part.at[0], middle, load_sem.at[4])
     keep.start()
-    for pair in sent:
-        for copy in pair:
-            copy.wait_send()
-    for copy in halos:
+    for copy in (*halos, *far_sent, *near_sent):
         copy.wait_send()
     keep.wait()
-    for copy in sent[-1]:
-        copy.wait_recv()
+    near_sent[-1].wait_recv()
+    far_sent[-1].wait_recv()
 
 
 def chain(count, tab, p_blocks, a_blocks):
     anywhere = pl.BlockSpec(memory_space=pl.ANY)
-    sums = [pltpu.VMEM((GROUP, width), BF16) for width in WIDTHS]
+    sums = [pltpu.VMEM((GROUP, width * BS), BF16) for width in (*FAR_WIDTH, *NEAR_WIDTH)]
     return pl.pallas_call(
         functools.partial(chain_kernel, count),
         out_shape=(
@@ -303,7 +308,6 @@
             pltpu.VMEM((ROWS, FRAME), F32),
             pltpu.VMEM((2, GROUP, FRAME), BF16),
             *sums,
-            *sums,
             pltpu.SemaphoreType.DMA((5,)),
             pltpu.SemaphoreType.DMA((2,)),
             pltpu.SemaphoreType.DMA((2,)),
@@ -318,13 +322,15 @@
     )(tab, p_blocks, a_blocks)
 
 
-def gather_kernel(left_ref, right_ref, middle_ref, out_ref, tot):
+def gather_kernel(far_ref, near_ref, middle_ref, out_ref, tot):
     odd = lax.rem(lax.axis_index("dom"), 2)
-    tot[:, :WIDE] = left_ref[...].astype(F32)
-    tot[:, WIDE:] = jnp.zeros((BS, TOTAL - WIDE), F32)
-    own = pl.ds(aligned((16 - 2 * odd) * BS), FRAME)
-    tot[:, own] += middle_ref[...].astype(F32)
-    tot[:, TOTAL - WIDE :] += right_ref[...].astype(F32)
+    tot[...] = jnp.zeros((BS, TOTAL), F32)
+    for ref, start, width in (
+        (far_ref, 18 * odd, WIDE),
+        (near_ref, 18 * (1 - odd), WIDE),
+        (middle_ref, 16 - 2 * odd, FRAME),
+    ):
+        tot[:, pl.ds(aligned(start * BS), width)] += ref[...].astype(F32)
     first = pl.program_id(0) + 1 - odd
     for start in range(NC + 1):
 
@@ -333,7 +339,7 @@
             out_ref[0] = tot[:, start * BS : (start + BAND) * BS]
 
 
-def gather(from_left, from_right, middle):
+def gather(from_far, from_near, middle):
     return pl.pallas_call(
         gather_kernel,
         out_shape=jax.ShapeDtypeStruct((NC, BS, BAND * BS), F32),
@@ -345,7 +351,7 @@
         ],
         out_specs=pl.BlockSpec((1, BS, BAND * BS), lambda i: (i, 0, 0)),
         scratch_shapes=[pltpu.VMEM((BS, TOTAL), F32)],
-    )(from_left, from_right, middle)
+    )(from_far, from_near, middle)
 
 
 def body(a_blocks, p_blocks, cols_a, cols_p):

time: 132 us -> 109 us (0.83)
  Pallas kernels: 129 us -> 106 us
    pallas_call x1, Pallas kernels: 123 us -> 100 us  [chain(): pl.pallas_call(functools.partial(chain_kernel, count), out_shape=(jax.Sha...]
where the time goes in v2:
time: 109 us; the launch traced here: 108 us
  Pallas kernels  106 us (97%)
  other arithmetic  2.5 us (2%)
    pallas_call x1, Pallas kernels, chain(): pl.pallas_call(functools.partial(chain_kernel, count), out_shape=(jax.Sha...  100 us
    pallas_call x1, Pallas kernels, gather(): pl.pallas_call(gather_kernel, out_shape=jax.ShapeDtypeStruct((NC, BS, BAN...  5.43 us

profile of v2, /device:TPU:0, one launch (start us, length us, event | category | flops | bytes accessed | tf_op | source)
XLA Modules:
  0.0 108.4 jit_solution(15964080969325685233)
XLA Ops:
  0.0 0.7 add_select_fusion.1
  0.7 0.1 select_reduce_fusion.1
  0.8 0.8 add_add_fusion
  1.7 0.1 copy.6
  1.7 0.2 select_reduce_fusion
  2.0 0.6 pad_add_fusion.tab
  2.6 100.3 %shard_map.46 = (bf16[192,3072]{1,0:T(8,128)(2,1)}, bf16[192,3072]{1,0:T(8,128)(2,1)}, bf16[192,2304]{1,0:T(8,128)(2,1)}) custom-call(s32[64,36]{1,0:T(8,128)} %pad_add_fusion.tab, bf16[24,64,1728]{2,1,0:T(8,128)(2,1)} %p_blocks.1, bf16[24,64,448]{2,1,0:T(8,128)(2,1)} %a_blocks.1), custom_call_target="tpu_custom_call" | custom-call | tf_op jit(solution)/shard_map/pallas_call | solution.py:289
  103.0 5.4 %shard_map.47 = f32[3,64,4032]{2,1,0:T(8,128)} custom-call(bf16[192,3072]{1,0:T(8,128)(2,1)} %get-tuple-element.8.far_ref, bf16[192,3072]{1,0:T(8,128)(2,1)} %get-tuple-element.9.near_ref, bf16[192,2304]{1,0:T(8,128)(2,1)} %get-tuple-element.10.middle_ref), custom_call_target="tpu_custom_call" | custom-call | tf_op jit(solution)/shard_map/pallas_call | solution.py:343
  (8 shorter events, 0.0 us)

commit v3 on v2

v3 whole, which is shorter than its diff:
```python
import functools

import jax
import jax.numpy as jnp
from jax import lax
from jax.experimental import pallas as pl
from jax.experimental.pallas import tpu as pltpu
from jax.sharding import PartitionSpec as P

BS = 64
KA = 7
KP = 27
AGG = 8
H = 15
NC = 3
NB = 24
WIN = 31
BAND = 63
REACH = 5
MESH = pl.DeviceIdType.MESH

ROWS = AGG * BS
FRAME = 36 * BS
WIDE = 48 * BS
FAR_WIDTH, FAR_SHIFT = [36, 38, 42, 44, 48], [0, 2, 6, 8, 12]
NEAR_WIDTH, NEAR_SHIFT = [36, 40, 42, 46, 48], [0, 4, 6, 10, 12]
GROUP = NC * BS
PIECE = 2
CHUNK = 768
FIRST = FRAME // CHUNK
F32 = jnp.float32
BF16 = jnp.bfloat16


def tables(cols_a, cols_p, device, count_agg):
    odd = lax.rem(device, 2)

    def wrapped(x, period):
        x = jnp.where(x < 0, x + period, x)
        return jnp.where(x >= period, x - period, x)

    def tile_of(target, blocks, tiles):
        rows = target.shape[0]
        spots = lax.broadcasted_iota(jnp.int32, (rows, 128), 1)
        found = jnp.full((rows, 128), blocks, jnp.int32)
        for order in range(blocks):
            found = jnp.where(target[:, order : order + 1] == spots, order, found)
        return ((found ^ spots) & 1) * tiles + (found >> 1)

    agg = lax.broadcasted_iota(jnp.int32, (NB, KP), 0) >> 3
    slot = wrapped(cols_p - (device * NC + agg) + H, count_agg)
    agg_a = lax.broadcasted_iota(jnp.int32, (NB, KA), 0) >> 3
    fine = wrapped(cols_a - (device * NC + agg_a - 1) * AGG, count_agg * AGG)
    return (
        tile_of(slot + agg + 1 + odd, KP, 14),
        tile_of(slot[:AGG] + (5 - odd), KP, 14),
        tile_of(slot[NB - AGG :] + (1 - odd), KP, 14),
        tile_of(fine, KA, 4),
    )


def swap_halves(x):
    return jnp.concatenate([x[:, BS:], x[:, :BS]], axis=1)


def dot(a, b):
    return jnp.dot(a, b, preferred_element_type=F32)


def aligned(value, multiple=128):
    return pl.multiple_of(value, multiple)


def doubled(src, first, dst, wide, tiles, begin=0, end=AGG):
    def step(e, _):
        rows = pl.ds(aligned(e * BS, BS), BS)
        for tile in range(tiles):
            if 128 * (tile + 1) <= wide:
                here = src[first + e, :, 128 * tile : 128 * tile + 128]
            else:
                here = jnp.concatenate([src[first + e, :, 128 * tile : wide], jnp.zeros((BS, BS), BF16)], axis=1)
            dst[tile, rows, :] = here
            dst[tiles + tile, rows, :] = swap_halves(here)
        return 0

    lax.fori_loop(begin, end, step, 0)


def place(tab, first, src, dst, dst_row, pairs, begin=0, end=AGG):
    low = lax.broadcasted_iota(jnp.int32, (BS, 128), 1) < BS

    def step(e, _):
        rows = pl.ds(aligned(e * BS, BS), BS)
        to = pl.ds(aligned(dst_row + e * BS, BS), BS)
        for pair in range(pairs):
            left = src[tab[first + e, 2 * pair], rows, :]
            right = src[tab[first + e, 2 * pair + 1], rows, :]
            dst[to, 128 * pair : 128 * pair + 128] = jnp.where(low, left, right)
        return 0

    lax.fori_loop(begin, end, step, 0)


def chain_kernel(count, cols_a, cols_p, p_blocks, a_blocks, from_far, from_near, middle, *scratch):
    tab_made, tab, raw, raw_a, halo, halo_tab, tab_here, p2, a2, ext, pt, ad, w, wf, part = scratch[:15]
    to_far = [*scratch[15 : 15 + REACH], from_near]
    to_near = [*scratch[15 + REACH : 15 + 2 * REACH], from_far]
    load_sem, halo_send, halo_recv, send_far, recv_far, send_near, recv_near = scratch[15 + 2 * REACH :]
    me = lax.axis_index("dom")
    odd = lax.rem(me, 2)
    far, near = lax.rem(me + count - 1 + 2 * odd, count), lax.rem(me + count + 1 - 2 * odd, count)
    far_agg, near_agg = 2 * odd, 2 - 2 * odd

    def load(agg, slot, sem):
        return pltpu.make_async_copy(p_blocks.at[pl.ds(AGG * agg, AGG)], raw.at[slot], load_sem.at[sem])

    loads = [load(far_agg, 0, 0), load(near_agg, 1, 1)]
    load_a = pltpu.make_async_copy(a_blocks, raw_a, load_sem.at[2])
    for copy in (*loads, load_a):
        copy.start()
    barrier = pltpu.get_barrier_semaphore()
    for neighbour in (far, near):
        pl.semaphore_signal(barrier, inc=1, device_id=(neighbour,), device_id_type=MESH)

    def remote(src, dst, send_sem, recv_sem, target):
        return pltpu.make_async_remote_copy(
            src_ref=src, dst_ref=dst, send_sem=send_sem, recv_sem=recv_sem, device_id=(target,), device_id_type=MESH
        )

    def halo_copies(side, target, agg):
        copies = [
            remote(
                tab_made.at[pl.ds(aligned(NB + 4 * agg, 8), AGG)],
                halo_tab.at[side],
                halo_send.at[side, AGG // PIECE],
                halo_recv.at[side, AGG // PIECE],
                target,
            )
        ]
        for piece in range(AGG // PIECE):
            copies.append(
                remote(
                    p_blocks.at[pl.ds(AGG * agg + PIECE * piece, PIECE)],
                    halo.at[side, pl.ds(PIECE * piece, PIECE)],
                    halo_send.at[side, piece],
                    halo_recv.at[side, piece],
                    target,
                )
            )
        return copies

    halos = [halo_copies(0, far, far_agg), halo_copies(1, near, near_agg)]

    def own(agg):
        place(tab, AGG * agg, p2, ext, ROWS + ROWS * agg, 18)

    def arrived(side, edge):
        halos[side][0].wait_recv()
        pltpu.make_async_copy(halo_tab.at[side], tab_here.at[side], load_sem.at[5 + side]).start()
        pltpu.make_async_copy(halo_tab.at[side], tab_here.at[side], load_sem.at[5 + side]).wait()
        for piece in range(AGG // PIECE):
            rows = PIECE * piece, PIECE * (piece + 1)
            halos[side][1 + piece].wait_recv()
            doubled(halo.at[side], 0, p2, KP * BS, 14, *rows)
            place(tab_here.at[side], 0, p2, ext, 4 * ROWS * edge, 18, *rows)

    at = 0
    for made in tables(cols_a[...].T, cols_p[...], me, NC * count):
        tab_made[at : at + made.shape[0], :] = made
        at += made.shape[0]
    load_tab = pltpu.make_async_copy(tab_made, tab, load_sem.at[7])
    load_tab.start()
    loads[0].wait()
    doubled(raw.at[0], 0, p2, KP * BS, 14)
    inner_load = load(1, 0, 3)
    inner_load.start()
    pl.semaphore_wait(barrier, 2)
    for copy in (*halos[0], *halos[1]):
        copy.start()
    load_tab.wait()
    own(far_agg)
    loads[1].wait()
    doubled(raw.at[1], 0, p2, KP * BS, 14)
    own(near_agg)
    inner_load.wait()
    doubled(raw.at[0], 0, p2, KP * BS, 14)
    own(1)
    load_a.wait()
    for agg in range(NC):
        doubled(raw_a, AGG * agg, a2, KA * BS, 4)
        place(tab, NB + 2 * AGG + AGG * agg, a2, ad, ROWS * agg, 12)

    for step in range(1, REACH):
        for buf, more, goes_right, before in (
            (to_far, 2 * BS, odd, NEAR_WIDTH[step - 1]),
            (to_near, 4 * BS, 1 - odd, FAR_WIDTH[step - 1]),
        ):
            buf[step][:, pl.ds(aligned(goes_right * before * BS), more)] = jnp.zeros((GROUP, more), BF16)

    def turn(tile):
        lanes = pl.ds(aligned(tile * 128), 128)
        for agg in range(NC):
            pt[lanes, ROWS * agg : ROWS * (agg + 1)] = ext[ROWS * (agg + 1) : ROWS * (agg + 2), lanes].T

    def chunks(body):
        def step(n, _):
            body(aligned(n * CHUNK))
            return 0

        lax.fori_loop(0, FRAME // CHUNK, step, 0)

    far_rows = pl.ds(aligned(far_agg * ROWS), ROWS)
    near_rows = pl.ds(aligned(near_agg * ROWS), ROWS)

    def inner(at):
        cols = pl.ds(at, CHUNK)
        w[ROWS : 2 * ROWS, cols] = dot(ad[ROWS : 2 * ROWS, :], ext[ROWS : 4 * ROWS, cols]).astype(BF16)
        wf[:, cols] = dot(
            ad[far_rows, pl.ds(aligned(ROWS * (1 - odd)), 2 * ROWS)],
            ext[pl.ds(aligned(ROWS + ROWS * odd), 2 * ROWS), cols],
        )

    def near_side(at):
        cols = pl.ds(at, CHUNK)
        whole = dot(ad[near_rows, :], ext[pl.ds(aligned(2 * ROWS * (1 - odd)), 3 * ROWS), cols])
        w[near_rows, cols] = whole.astype(BF16)

    def far_side(at):
        cols = pl.ds(at, CHUNK)
        more = dot(
            ad[far_rows, pl.ds(aligned(2 * ROWS * odd), ROWS)],
            ext[pl.ds(aligned(4 * ROWS * odd), ROWS), cols],
        )
        w[far_rows, cols] = (wf[:, cols] + more).astype(BF16)

    def product(group, at):
        rows = pl.ds(aligned((NC * group + 1 + odd) * BS, BS), GROUP)
        return dot(pt[rows, :], w[:, pl.ds(at, CHUNK)]).astype(BF16)

    def send(step, far_side, at=0, width=None, sem=None):
        buf, lands = (to_far, to_near) if far_side else (to_near, to_far)
        width = (FAR_WIDTH if far_side else NEAR_WIDTH)[step] * BS if width is None else width
        sem = step + FIRST - 1 if sem is None else sem
        grows = 0 if step == REACH - 1 else (4 * BS if far_side else 2 * BS)
        goes_left = 1 - odd if far_side else odd
        copy = remote(
            buf[step].at[:, pl.ds(at, width)],
            lands[step + 1].at[:, pl.ds(aligned(goes_left * grows + at), width)],
            (send_far if far_side else send_near).at[sem],
            (recv_far if far_side else recv_near).at[sem],
            far if far_side else near,
        )
        copy.start()
        return [copy]

    def far_product(step, at):
        return product(REACH + (REACH - step) * (2 * odd - 1), at)

    def near_product(step, at):
        return product(REACH - (REACH - step) * (2 * odd - 1), at)

    def add(buf, shift, side):
        def some(at):
            cols = pl.ds(aligned(at + shift * BS), CHUNK)
            summed = buf[:, cols].astype(F32) + part[side, :, pl.ds(at, CHUNK)].astype(F32)
            buf[:, cols] = summed.astype(BF16)

        chunks(some)

    def far_first(at):
        to_far[0][:, pl.ds(at, CHUNK)] = far_product(0, at)

    def near_first(at):
        to_near[0][:, pl.ds(at, CHUNK)] = near_product(0, at)

    for tile in range(2):
        turn(tile + 16 * odd)
        turn(tile + 15 - 14 * odd)
        turn(tile + 2 + 12 * odd)
    arrived(1, 1 - odd)

    def ready(at):
        inner(at)
        near_side(at)

    def some_chunks(n, _):
        ready(aligned(n * CHUNK))
        return 0

    lax.fori_loop(0, FIRST - 1, some_chunks, 0)
    arrived(0, odd)
    far_sent, near_sent = [[]], [[]]
    for n in range(FIRST):
        at = n * CHUNK
        if n == FIRST - 1:
            ready(at)
        far_side(at)
        far_first(at)
        far_sent[0] += send(0, True, at, CHUNK, n)
        near_first(at)
        near_sent[0] += send(0, False, at, CHUNK, n)

    def turn_all(tile, _):
        turn(tile)
        return 0

    for step in range(REACH):
        if step == 1:
            lax.fori_loop(0, FRAME // 128, turn_all, 0)

        def prepare(at):
            cols = pl.ds(at, CHUNK)
            if step > 0:
                part[1, :, cols] = near_product(step, at)
            if step + 1 < REACH:
                part[0, :, cols] = far_product(step + 1, at)

        chunks(prepare)
        if step > 0:
            for copy in far_sent[step - 1]:
                copy.wait_recv()
            add(to_near[step], NEAR_SHIFT[step] * (1 - odd), 1)
            near_sent.append(send(step, False))
        if step + 1 < REACH:
            for copy in near_sent[step]:
                copy.wait_recv()
            add(to_far[step + 1], FAR_SHIFT[step + 1] * odd, 0)
            far_sent.append(send(step + 1, True))

    def centre(at):
        part[0, :, pl.ds(at, CHUNK)] = product(REACH, at)

    chunks(centre)
    keep = pltpu.make_async_copy(part.at[0], middle, load_sem.at[4])
    keep.start()
    for copies in (*halos, *far_sent, *near_sent):
        for copy in copies:
            copy.wait_send()
    keep.wait()
    near_sent[-1][0].wait_recv()
    far_sent[-1][0].wait_recv()


def chain(count, cols_a, cols_p, p_blocks, a_blocks):
    anywhere = pl.BlockSpec(memory_space=pl.ANY)
    sums = [pltpu.VMEM((GROUP, width * BS), BF16) for width in (*FAR_WIDTH, *NEAR_WIDTH)]
    return pl.pallas_call(
        functools.partial(chain_kernel, count),
        out_shape=(
            jax.ShapeDtypeStruct((GROUP, WIDE), BF16),
            jax.ShapeDtypeStruct((GROUP, WIDE), BF16),
            jax.ShapeDtypeStruct((GROUP, FRAME), BF16),
        ),
        in_specs=[pl.BlockSpec(memory_space=pltpu.VMEM), pl.BlockSpec(memory_space=pltpu.VMEM), anywhere, anywhere],
        out_specs=[anywhere] * 3,
        scratch_shapes=[
            pltpu.VMEM((2 * NB + 2 * AGG, 128), jnp.int32),
            pltpu.SMEM((2 * NB + 2 * AGG, 128), jnp.int32),
            pltpu.VMEM((2, AGG, BS, KP * BS), BF16),
            pltpu.VMEM((NB, BS, KA * BS), BF16),
            pltpu.VMEM((2, AGG, BS, KP * BS), BF16),
            pltpu.VMEM((2, AGG, 128), jnp.int32),
            pltpu.SMEM((2, AGG, 128), jnp.int32),
            pltpu.VMEM((2 * 14, ROWS, 128), BF16),
            pltpu.VMEM((2 * 4, ROWS, 128), BF16),
            pltpu.VMEM((5 * ROWS, FRAME), BF16),
            pltpu.VMEM((FRAME, 3 * ROWS), BF16),
            pltpu.VMEM((3 * ROWS, 3 * ROWS), BF16),
            pltpu.VMEM((3 * ROWS, FRAME), BF16),
            pltpu.VMEM((ROWS, FRAME), F32),
            pltpu.VMEM((2, GROUP, FRAME), BF16),
            *sums,
            pltpu.SemaphoreType.DMA((8,)),
            pltpu.SemaphoreType.DMA((2, AGG // PIECE + 1)),
            pltpu.SemaphoreType.DMA((2, AGG // PIECE + 1)),
            pltpu.SemaphoreType.DMA((REACH + FIRST - 1,)),
            pltpu.SemaphoreType.DMA((REACH + FIRST - 1,)),
            pltpu.SemaphoreType.DMA((REACH + FIRST - 1,)),
            pltpu.SemaphoreType.DMA((REACH + FIRST - 1,)),
        ],
        compiler_params=pltpu.CompilerParams(
            collective_id=0, has_side_effects=True, vmem_limit_bytes=63 * 2**20
        ),
    )(cols_a, cols_p, p_blocks, a_blocks)


def gather_kernel(far_ref, near_ref, middle_ref, out_ref):
    odd = lax.rem(lax.axis_index("dom"), 2)
    row = pl.program_id(0)

    def write(parity, first):
        parts = [
            (near_ref if parity else far_ref, 0, 48),
            (middle_ref, 16 - 2 * parity, 52 - 2 * parity),
            (far_ref if parity else near_ref, 18, 66),
        ]
        edges = sorted({edge for _, begin, end in parts for edge in (begin, end)})
        for begin, end in zip(edges[:-1], edges[1:]):
            terms = [
                ref[:, (begin - left) * BS : (end - left) * BS].astype(F32)
                for ref, left, right in parts
                if left <= begin and end <= right
            ]
            value = functools.reduce(jnp.add, terms)
            low, high = max(begin, first), min(end, first + BAND)
            out_ref[0, :, (low - first) * BS : (high - first) * BS] = value[:, (low - begin) * BS : (high - begin) * BS]

    for parity in (0, 1):
        for at in range(NC):

            @pl.when((odd == parity) & (row == at))
            def _():
                write(parity, at + 1 - parity)


def gather(from_far, from_near, middle):
    return pl.pallas_call(
        gather_kernel,
        out_shape=jax.ShapeDtypeStruct((NC, BS, BAND * BS), F32),
        grid=(NC,),
        in_specs=[
            pl.BlockSpec((BS, WIDE), lambda i: (i, 0)),
            pl.BlockSpec((BS, WIDE), lambda i: (i, 0)),
            pl.BlockSpec((BS, FRAME), lambda i: (i, 0)),
        ],
        out_specs=pl.BlockSpec((1, BS, BAND * BS), lambda i: (i, 0, 0)),
    )(from_far, from_near, middle)


def body(a_blocks, p_blocks, cols_a, cols_p):
    count = lax.axis_size("dom")
    return gather(*chain(count, cols_a.T, cols_p, p_blocks, a_blocks))


def solution(mesh):
    in_specs = (P("dom", None, None), P("dom", None, None), P("dom", None), P("dom", None))
    out_specs = P("dom", None, None)
    return jax.shard_map(body, mesh=mesh, in_specs=in_specs, out_specs=out_specs, check_vma=False)
```

time: 109 us -> 102 us (0.936)
  Pallas kernels: 106 us -> 102 us
  other arithmetic: 2.5 us -> 0 us
    pallas_call x1, Pallas kernels: 100 us -> 97.3 us  [chain(): pl.pallas_call(functools.partial(chain_kernel, count), out_shape=(jax.Sha...]
where the time goes in v3:
time: 102 us
  Pallas kernels  102 us (100%)
    pallas_call x1, Pallas kernels, chain(): pl.pallas_call(functools.partial(chain_kernel, count), out_shape=(jax.Sha...  97.3 us
    pallas_call x1, Pallas kernels, gather(): pl.pallas_call(gather_kernel, out_shape=jax.ShapeDtypeStruct((NC, BS, BAN...  4.75 us

profile of v3, /device:TPU:0, one launch (start us, length us, event | category | flops | bytes accessed | tf_op | source)
XLA Modules:
  0.0 102.0 jit_solution(13549438680912845241)
XLA Ops:
  0.0 97.3 %shard_map.46 = (bf16[192,3072]{1,0:T(8,128)(2,1)}, bf16[192,3072]{1,0:T(8,128)(2,1)}, bf16[192,2304]{1,0:T(8,128)(2,1)}) custom-call(s32[7,24]{1,0:T(8,128)} %bitcast.1, s32[24,27]{1,0:T(8,128)} %cols_p.1, bf16[24,64,1728]{2,1,0:T(8,128)(2,1)} %p_blocks.1, bf16[24,64,448]{2,1,0:T(8,128)(2,1)} %a_blocks.1), custom_call_target="tpu_custom_call" | custom-call | tf_op jit(solution)/shard_map/pallas_call | solution.py:347
  97.3 4.8 %shard_map.47 = f32[3,64,4032]{2,1,0:T(8,128)} custom-call(bf16[192,3072]{1,0:T(8,128)(2,1)} %get-tuple-element.8.far_ref, bf16[192,3072]{1,0:T(8,128)(2,1)} %get-tuple-element.9.near_ref, bf16[192,2304]{1,0:T(8,128)(2,1)} %get-tuple-element.10.middle_ref), custom_call_target="tpu_custom_call" | custom-call | tf_op jit(solution)/shard_map/pallas_call | solution.py:417

commit v4 on v3

--- a/solution.py
+++ b/solution.py
@@ -287,13 +287,11 @@
         ready(aligned(n * CHUNK))
         return 0
 
-    lax.fori_loop(0, FIRST - 1, some_chunks, 0)
+    lax.fori_loop(0, FIRST, some_chunks, 0)
     arrived(0, odd)
     far_sent, near_sent = [[]], [[]]
     for n in range(FIRST):
         at = n * CHUNK
-        if n == FIRST - 1:
-            ready(at)
         far_side(at)
         far_first(at)
         far_sent[0] += send(0, True, at, CHUNK, n)
@@ -384,11 +382,23 @@
     )(cols_a, cols_p, p_blocks, a_blocks)
 
 
-def gather_kernel(far_ref, near_ref, middle_ref, out_ref):
+def gather_kernel(from_far, from_near, middle, out, far_ref, near_ref, middle_ref, out_ref, load_sem, store_sem):
     odd = lax.rem(lax.axis_index("dom"), 2)
-    row = pl.program_id(0)
-
-    def write(parity, first):
+    pairs = ((from_far, far_ref), (from_near, near_ref), (middle, middle_ref))
+    loads = [
+        [
+            pltpu.make_async_copy(src.at[pl.ds(BS * row, BS)], dst.at[row], load_sem.at[row, kind])
+            for kind, (src, dst) in enumerate(pairs)
+        ]
+        for row in range(NC)
+    ]
+    stores = [pltpu.make_async_copy(out_ref.at[row], out.at[row], store_sem.at[row]) for row in range(NC)]
+    for copies in loads:
+        for copy in copies:
+            copy.start()
+
+    def write(row, parity):
+        first = row + 1 - parity
         parts = [
             (near_ref if parity else far_ref, 0, 48),
             (middle_ref, 16 - 2 * parity, 52 - 2 * parity),
@@ -397,33 +407,40 @@
         edges = sorted({edge for _, begin, end in parts for edge in (begin, end)})
         for begin, end in zip(edges[:-1], edges[1:]):
             terms = [
-                ref[:, (begin - left) * BS : (end - left) * BS].astype(F32)
+                ref[row, :, (begin - left) * BS : (end - left) * BS].astype(F32)
                 for ref, left, right in parts
                 if left <= begin and end <= right
             ]
             value = functools.reduce(jnp.add, terms)
             low, high = max(begin, first), min(end, first + BAND)
-            out_ref[0, :, (low - first) * BS : (high - first) * BS] = value[:, (low - begin) * BS : (high - begin) * BS]
-
-    for parity in (0, 1):
-        for at in range(NC):
-
-            @pl.when((odd == parity) & (row == at))
-            def _():
-                write(parity, at + 1 - parity)
+            out_ref[row, :, (low - first) * BS : (high - first) * BS] = value[:, (low - begin) * BS : (high - begin) * BS]
+
+    for row in range(NC):
+        for copy in loads[row]:
+            copy.wait()
+        for parity in (0, 1):
+            pl.when(odd == parity)(functools.partial(write, row, parity))
+        stores[row].start()
+    for copy in stores:
+        copy.wait()
 
 
 def gather(from_far, from_near, middle):
+    anywhere = pl.BlockSpec(memory_space=pl.ANY)
     return pl.pallas_call(
         gather_kernel,
         out_shape=jax.ShapeDtypeStruct((NC, BS, BAND * BS), F32),
-        grid=(NC,),
-        in_specs=[
-            pl.BlockSpec((BS, WIDE), lambda i: (i, 0)),
-            pl.BlockSpec((BS, WIDE), lambda i: (i, 0)),
-            pl.BlockSpec((BS, FRAME), lambda i: (i, 0)),
+        in_specs=[anywhere] * 3,
+        out_specs=anywhere,
+        scratch_shapes=[
+            pltpu.VMEM((NC, BS, WIDE), BF16),
+            pltpu.VMEM((NC, BS, WIDE), BF16),
+            pltpu.VMEM((NC, BS, FRAME), BF16),
+            pltpu.VMEM((NC, BS, BAND * BS), F32),
+            pltpu.SemaphoreType.DMA((NC, 3)),
+            pltpu.SemaphoreType.DMA((NC,)),
         ],
-        out_specs=pl.BlockSpec((1, BS, BAND * BS), lambda i: (i, 0, 0)),
+        compiler_params=pltpu.CompilerParams(vmem_limit_bytes=62 * 2**20),
     )(from_far, from_near, middle)
 
 

time: 102 us -> 99.3 us (0.974)
  Pallas kernels: 102 us -> 98.9 us
    pallas_call x1, Pallas kernels: 97.3 us -> 95.7 us  [chain(): pl.pallas_call(functools.partial(chain_kernel, count), out_shape=(jax.Sha...]
    pallas_call x1, Pallas kernels: 4.75 us -> 3.24 us  [gather(): pl.pallas_call(gather_kernel, out_shape=jax.ShapeDtypeStruct((NC, BS, BAN...]
where the time goes in v4:
time: 99.3 us; the launch traced here: 99.1 us
  Pallas kernels  98.9 us (100%)
    pallas_call x1, Pallas kernels, chain(): pl.pallas_call(functools.partial(chain_kernel, count), out_shape=(jax.Sha...  95.7 us
    pallas_call x1, Pallas kernels, gather(): pl.pallas_call(gather_kernel, out_shape=jax.ShapeDtypeStruct((NC, BS, BAN...  3.24 us

profile of v4, /device:TPU:0, one launch (start us, length us, event | category | flops | bytes accessed | tf_op | source)
XLA Modules:
  0.0 99.1 jit_solution(2321172202142357829)
XLA Ops:
  0.0 95.7 %shard_map.46 = (bf16[192,3072]{1,0:T(8,128)(2,1)}, bf16[192,3072]{1,0:T(8,128)(2,1)}, bf16[192,2304]{1,0:T(8,128)(2,1)}) custom-call(s32[7,24]{1,0:T(8,128)} %bitcast.1, s32[24,27]{1,0:T(8,128)} %cols_p.1, bf16[24,64,1728]{2,1,0:T(8,128)(2,1)} %p_blocks.1, bf16[24,64,448]{2,1,0:T(8,128)(2,1)} %a_blocks.1), custom_call_target="tpu_custom_call" | custom-call | tf_op jit(solution)/shard_map/pallas_call | solution.py:345
  95.7 3.2 %shard_map.47 = f32[3,64,4032]{2,1,0:T(8,128)} custom-call(bf16[192,3072]{1,0:T(8,128)(2,1)} %get-tuple-element.8.from_far, bf16[192,3072]{1,0:T(8,128)(2,1)} %get-tuple-element.9.from_near, bf16[192,2304]{1,0:T(8,128)(2,1)} %get-tuple-element.10.middle), custom_call_target="tpu_custom_call" | custom-call | tf_op jit(solution)/shard_map/pallas_call | solution.py:430

commit v5 on v4

--- a/solution.py
+++ b/solution.py
@@ -102,10 +102,10 @@
 
 
 def chain_kernel(count, cols_a, cols_p, p_blocks, a_blocks, from_far, from_near, middle, *scratch):
-    tab_made, tab, raw, raw_a, halo, halo_tab, tab_here, p2, a2, ext, pt, ad, w, wf, part = scratch[:15]
-    to_far = [*scratch[15 : 15 + REACH], from_near]
-    to_near = [*scratch[15 + REACH : 15 + 2 * REACH], from_far]
-    load_sem, halo_send, halo_recv, send_far, recv_far, send_near, recv_near = scratch[15 + 2 * REACH :]
+    here_a, here_p, tab_made, tab, raw, raw_a, halo, halo_tab, tab_here, p2, a2, ext, pt, ad, w, wf, part = scratch[:17]
+    to_far = [*scratch[17 : 17 + REACH], from_near]
+    to_near = [*scratch[17 + REACH : 17 + 2 * REACH], from_far]
+    load_sem, halo_send, halo_recv, send_far, recv_far, send_near, recv_near = scratch[17 + 2 * REACH :]
     me = lax.axis_index("dom")
     odd = lax.rem(me, 2)
     far, near = lax.rem(me + count - 1 + 2 * odd, count), lax.rem(me + count + 1 - 2 * odd, count)
@@ -114,13 +114,17 @@
     def load(agg, slot, sem):
         return pltpu.make_async_copy(p_blocks.at[pl.ds(AGG * agg, AGG)], raw.at[slot], load_sem.at[sem])
 
-    loads = [load(far_agg, 0, 0), load(near_agg, 1, 1)]
-    load_a = pltpu.make_async_copy(a_blocks, raw_a, load_sem.at[2])
-    for copy in (*loads, load_a):
-        copy.start()
     barrier = pltpu.get_barrier_semaphore()
     for neighbour in (far, near):
         pl.semaphore_signal(barrier, inc=1, device_id=(neighbour,), device_id_type=MESH)
+    load_cols = [
+        pltpu.make_async_copy(cols_a, here_a, load_sem.at[8]),
+        pltpu.make_async_copy(cols_p, here_p, load_sem.at[9]),
+    ]
+    loads = [load(far_agg, 0, 0), load(near_agg, 1, 1)]
+    load_a = pltpu.make_async_copy(a_blocks, raw_a, load_sem.at[2])
+    for copy in (*load_cols, *loads, load_a):
+        copy.start()
 
     def remote(src, dst, send_sem, recv_sem, target):
         return pltpu.make_async_remote_copy(
@@ -164,8 +168,10 @@
             doubled(halo.at[side], 0, p2, KP * BS, 14, *rows)
             place(tab_here.at[side], 0, p2, ext, 4 * ROWS * edge, 18, *rows)
 
+    for copy in load_cols:
+        copy.wait()
     at = 0
-    for made in tables(cols_a[...].T, cols_p[...], me, NC * count):
+    for made in tables(here_a[...].T, here_p[...], me, NC * count):
         tab_made[at : at + made.shape[0], :] = made
         at += made.shape[0]
     load_tab = pltpu.make_async_copy(tab_made, tab, load_sem.at[7])
@@ -349,9 +355,11 @@
             jax.ShapeDtypeStruct((GROUP, WIDE), BF16),
             jax.ShapeDtypeStruct((GROUP, FRAME), BF16),
         ),
-        in_specs=[pl.BlockSpec(memory_space=pltpu.VMEM), pl.BlockSpec(memory_space=pltpu.VMEM), anywhere, anywhere],
+        in_specs=[anywhere] * 4,
         out_specs=[anywhere] * 3,
         scratch_shapes=[
+            pltpu.VMEM((KA, NB), jnp.int32),
+            pltpu.VMEM((NB, KP), jnp.int32),
             pltpu.VMEM((2 * NB + 2 * AGG, 128), jnp.int32),
             pltpu.SMEM((2 * NB + 2 * AGG, 128), jnp.int32),
             pltpu.VMEM((2, AGG, BS, KP * BS), BF16),
@@ -368,7 +376,7 @@
             pltpu.VMEM((ROWS, FRAME), F32),
             pltpu.VMEM((2, GROUP, FRAME), BF16),
             *sums,
-            pltpu.SemaphoreType.DMA((8,)),
+            pltpu.SemaphoreType.DMA((10,)),
             pltpu.SemaphoreType.DMA((2, AGG // PIECE + 1)),
             pltpu.SemaphoreType.DMA((2, AGG // PIECE + 1)),
             pltpu.SemaphoreType.DMA((REACH + FIRST - 1,)),

time: 99.3 us -> 98.5 us (level)
  no operation moved by 1% of the time
where the time goes in v5:
time: 98.5 us; the launch traced here: 98.4 us
  Pallas kernels  98.2 us (100%)
    pallas_call x1, Pallas kernels, chain(): pl.pallas_call(functools.partial(chain_kernel, count), out_shape=(jax.Sha...  95 us
    pallas_call x1, Pallas kernels, gather(): pl.pallas_call(gather_kernel, out_shape=jax.ShapeDtypeStruct((NC, BS, BAN...  3.24 us

profile of v5, /device:TPU:0, one launch (start us, length us, event | category | flops | bytes accessed | tf_op | source)
XLA Modules:
  0.0 98.4 jit_solution(18040907326995081482)
XLA Ops:
  0.0 95.0 %shard_map.46 = (bf16[192,3072]{1,0:T(8,128)(2,1)}, bf16[192,3072]{1,0:T(8,128)(2,1)}, bf16[192,2304]{1,0:T(8,128)(2,1)}) custom-call(s32[7,24]{1,0:T(8,128)} %bitcast.1, s32[24,27]{1,0:T(8,128)} %cols_p.1, bf16[24,64,1728]{2,1,0:T(8,128)(2,1)} %p_blocks.1, bf16[24,64,448]{2,1,0:T(8,128)(2,1)} %a_blocks.1), custom_call_target="tpu_custom_call" | custom-call | tf_op jit(solution)/shard_map/pallas_call | solution.py:351
  95.0 3.2 %shard_map.47 = f32[3,64,4032]{2,1,0:T(8,128)} custom-call(bf16[192,3072]{1,0:T(8,128)(2,1)} %get-tuple-element.8.from_far, bf16[192,3072]{1,0:T(8,128)(2,1)} %get-tuple-element.9.from_near, bf16[192,2304]{1,0:T(8,128)(2,1)} %get-tuple-element.10.middle), custom_call_target="tpu_custom_call" | custom-call | tf_op jit(solution)/shard_map/pallas_call | solution.py:438

commit v6 on v5

--- a/solution.py
+++ b/solution.py
@@ -25,7 +25,7 @@
 FAR_WIDTH, FAR_SHIFT = [36, 38, 42, 44, 48], [0, 2, 6, 8, 12]
 NEAR_WIDTH, NEAR_SHIFT = [36, 40, 42, 46, 48], [0, 4, 6, 10, 12]
 GROUP = NC * BS
-PIECE = 2
+PIECE = 1
 CHUNK = 768
 FIRST = FRAME // CHUNK
 F32 = jnp.float32

time: 98.5 us -> 98.3 us (level)
  no operation moved by 1% of the time
where the time goes in v6:
time: 98.3 us; the launch traced here: 98.1 us
  Pallas kernels  98 us (100%)
    pallas_call x1, Pallas kernels, chain(): pl.pallas_call(functools.partial(chain_kernel, count), out_shape=(jax.Sha...  94.7 us
    pallas_call x1, Pallas kernels, gather(): pl.pallas_call(gather_kernel, out_shape=jax.ShapeDtypeStruct((NC, BS, BAN...  3.24 us

profile of v6, /device:TPU:0, one launch (start us, length us, event | category | flops | bytes accessed | tf_op | source)
XLA Modules:
  0.0 98.1 jit_solution(12719290683994990367)
XLA Ops:
  0.0 94.7 %shard_map.46 = (bf16[192,3072]{1,0:T(8,128)(2,1)}, bf16[192,3072]{1,0:T(8,128)(2,1)}, bf16[192,2304]{1,0:T(8,128)(2,1)}) custom-call(s32[7,24]{1,0:T(8,128)} %bitcast.1, s32[24,27]{1,0:T(8,128)} %cols_p.1, bf16[24,64,1728]{2,1,0:T(8,128)(2,1)} %p_blocks.1, bf16[24,64,448]{2,1,0:T(8,128)(2,1)} %a_blocks.1), custom_call_target="tpu_custom_call" | custom-call | tf_op jit(solution)/shard_map/pallas_call | solution.py:351
  94.7 3.2 %shard_map.47 = f32[3,64,4032]{2,1,0:T(8,128)} custom-call(bf16[192,3072]{1,0:T(8,128)(2,1)} %get-tuple-element.8.from_far, bf16[192,3072]{1,0:T(8,128)(2,1)} %get-tuple-element.9.from_near, bf16[192,2304]{1,0:T(8,128)(2,1)} %get-tuple-element.10.middle), custom_call_target="tpu_custom_call" | custom-call | tf_op jit(solution)/shard_map/pallas_call | solution.py:438
